TPU v7x, 32 devices: a whole 2x2x4 slice. The times are simulated.
32 devices in a mesh: stn: 8 (over z, x), chan: 4 (over y, core).
Axes of the slice: x: 2, y: 2, z: 4, core: 2. Of those that a mesh axis runs over, the one named last changes fastest.
Arguments:
- samples: bfloat16 [64, 17, 2, 8192], P(('stn', 'chan')), may hold values from -6 to 6
- keeper: int32 [8, 8], replicated, may hold values from 0 to 1, as said below
Outputs:
- visibilities: bfloat16 [64, 2, 4096, 40], P('stn', None, 'chan')
Inputs may be any that keep to these rules, and one draw needn't show every extreme that they name: keeper[g, g] is 1; for g != h with d = (g - h) mod 8: keeper[g, h] is 1 where 0 < d < 4, 0 where d > 4, and at d = 4 exactly one of keeper[g, h] and keeper[h, g] is 1, which one drawn for each such pair; half of the rows hold 5 ones, the others 5 - 1.
All inputs are finite; a program needn't handle non-finite values.
Results may differ from a plain program's by a relative error of at most 0.0077.
Values may be sent and summed in bfloat16 or wider, within the bound.
A program may use at most 192 MiB of HBM per device.

v0:
```python
import math
import jax
import jax.numpy as jnp
from jax import lax
from jax.sharding import PartitionSpec as P

NFFT = 8192
TAPS = 16
CH_WIN = 1024
DFT_BLOCK = 256


def from_behind(value, axis, by):
    devices = lax.axis_size(axis)
    return lax.ppermute(value, axis, [(i, (i + by) % devices) for i in range(devices)])


def taps_table():
    pos = jnp.arange(TAPS * NFFT).astype(jnp.float32)
    shifted = (pos + 0.5) / NFFT - TAPS / 2.0
    window = 0.5 - 0.5 * jnp.cos(2.0 * math.pi * (pos + 0.5) / (TAPS * NFFT))
    return (jnp.sinc(shifted) * window).reshape(TAPS, NFFT)


def twiddles(width):
    index_n = jnp.arange(NFFT, dtype=jnp.int32)[:, None]
    index_k = jnp.arange(width, dtype=jnp.int32)[None, :]
    phase = (index_n * index_k % NFFT).astype(jnp.float32) * (2.0 * math.pi / NFFT)
    cosines = jnp.cos(phase).astype(jnp.bfloat16)
    sines = jnp.sin(phase).astype(jnp.bfloat16)
    upper = jnp.concatenate([cosines, -sines], axis=1)
    lower = jnp.concatenate([sines, cosines], axis=1)
    return jnp.concatenate([upper, lower], axis=0)


def rotations(ch_tot, width):
    blocks = ch_tot // width
    index_n = jnp.arange(NFFT, dtype=jnp.int32)[None, :]
    index_b = jnp.arange(blocks, dtype=jnp.int32)[:, None]
    phase = (index_n * index_b * width % NFFT).astype(jnp.float32) * (2.0 * math.pi / NFFT)
    return (jnp.cos(phase), jnp.sin(phase))


def channelise(block, taps, table, cos_rot, sin_rot, ch_tot):
    frames = block.shape[1] - TAPS + 1
    count = block.shape[0]
    width = table.shape[1] // 2
    blocks = ch_tot // width
    total = taps[0] * block[:, 0:frames].astype(jnp.float32)
    for tap in range(1, TAPS):
        total = total + taps[tap] * block[:, tap : tap + frames].astype(jnp.float32)
    real_part = total[:, :, 0][None]
    imag_part = total[:, :, 1][None]
    cosine = cos_rot[:, None, None, :]
    sine = sin_rot[:, None, None, :]
    rot_real = real_part * cosine + imag_part * sine
    rot_imag = imag_part * cosine - real_part * sine
    lhs = jnp.stack([rot_real, rot_imag], axis=3).astype(jnp.bfloat16)
    lhs = lhs.reshape(blocks * count * frames, 2 * NFFT)
    spectrum = jnp.dot(lhs, table, preferred_element_type=jnp.float32) * (1.0 / math.sqrt(NFFT))
    spectrum = spectrum.astype(jnp.bfloat16).reshape(blocks, count, frames, 2, width)
    spectrum = jnp.transpose(spectrum, (1, 0, 4, 3, 2))
    return spectrum.reshape(count, ch_tot, 2, frames)


def correlate(own, others, frames):
    half = others.shape[2] // 2
    turned = jnp.concatenate([-others[:, :, half:], others[:, :, :half]], axis=2)
    rhs = jnp.concatenate([others, turned], axis=0)
    product = lax.dot_general(
        own, rhs, (((2,), (2,)), ((1,), (1,))), preferred_element_type=jnp.float32
    )
    rows = others.shape[0]
    product = product.reshape(product.shape[0], product.shape[1], 2, rows)
    return jnp.transpose(product, (1, 2, 0, 3)) / frames


def slot_table(keep_rows, keep_slots):
    ranking = jnp.cumsum(keep_rows, axis=1) - 1
    slot_index = jnp.arange(keep_slots, dtype=jnp.int32)
    matched = (keep_rows[:, :, None] == 1) & (ranking[:, :, None] == slot_index[None, None, :])
    column_ids = jnp.arange(keep_rows.shape[1], dtype=jnp.int32)
    slot_column = jnp.sum(jnp.where(matched, column_ids[None, :, None], 0), axis=1)
    filled = jnp.any(matched, axis=1)
    return (slot_column, filled)


def per_device(samples, keeper):
    n_chan = lax.axis_size("chan")
    n_stn = lax.axis_size("stn")
    ch_tot = CH_WIN * n_chan
    frames = samples.shape[1] - TAPS + 1
    cos_rot, sin_rot = rotations(ch_tot, DFT_BLOCK)
    spectrum = channelise(samples, taps_table(), twiddles(DFT_BLOCK), cos_rot, sin_rot, ch_tot)
    local = lax.all_to_all(spectrum, "chan", split_axis=1, concat_axis=0, tiled=True)
    group_in = local.shape[0]
    own = local.reshape(group_in, CH_WIN, 2 * frames)
    keep_slots = n_stn // 2 + 1
    group_index = lax.axis_index("stn")
    row_keep = jnp.take(keeper, group_index, axis=0)
    slot_column, filled = slot_table(row_keep[None], keep_slots)
    slot_column = slot_column[0]
    filled = filled[0]
    nothing = jnp.zeros((), jnp.bfloat16)
    half = n_stn // 2
    stacked = own[None]
    stride = 1
    while stride < half:
        moved = from_behind(stacked, "stn", stride)
        stacked = jnp.concatenate([stacked, moved], axis=0)
        stride = stride * 2
    far_group = from_behind(own, "stn", half)
    partners = jnp.concatenate([stacked, far_group[None]], axis=0)
    partners = partners.reshape((half + 1) * group_in, CH_WIN, 2 * frames)
    tiles = correlate(own, partners, frames).astype(jnp.bfloat16)
    tiles = tiles.reshape(group_in, 2, CH_WIN, half + 1, group_in)
    slot_distance = jnp.minimum((group_index - slot_column) % n_stn, half)
    picked = jnp.take(tiles, slot_distance, axis=3)
    picked = jnp.where(filled[None, None, None, :, None], picked, nothing)
    return picked.reshape(group_in, 2, CH_WIN, keep_slots * group_in)


def solution(mesh):
    placed = (P(("stn", "chan"), None, None, None), P())
    return jax.shard_map(
        per_device,
        mesh=mesh,
        in_specs=placed,
        out_specs=P("stn", None, "chan", None),
        check_vma=False,
    )
```

profile of v0, /device:TPU:0, one launch (start us, length us, event | category | flops | bytes accessed | tf_op | source)
XLA Modules:
  0.0 166.4 jit_solution(14174221383164325046)
XLA Ops:
  0.0 2.4 %fusion.29 = f32[131072]{0:T(1024)S(1)} fusion(), kind=kLoop, calls=%fused_computation.45 | loop fusion | flops 5373952 | bytes 524288 | tf_op jit(solution)/shard_map/mul | solution.py:22
  2.4 2.1 %fusion.41 = (f32[16,8192]{1,0:T(8,128)S(1)}, f32[16,8192]{1,0:T(8,128)S(1)}) fusion(), kind=kLoop, calls=%fused_computation.65 | loop fusion | flops 1966080 | bytes 1048576 | tf_op jit(solution)/shard_map/sin | solution.py:41
  4.5 35.0 %sine_convert_fusion = (bf16[8192,256]{1,0:T(8,128)(2,1)}, bf16[8192,256]{1,0:T(8,128)(2,1)}) fusion(), kind=kLoop, calls=%fused_computation.15 | loop fusion | flops 33554432 | bytes 8388608 | tf_op jit(solution)/shard_map/convert_element_type | solution.py:30
  39.5 0.0 copy-start
  39.5 32.3 %fusion.14 = bf16[8192,256]{1,0:T(8,128)(2,1)} fusion(), kind=kLoop, calls=%fused_computation.24 | loop fusion | flops 37748736 | bytes 4194304 | tf_op jit(solution)/shard_map/neg | solution.py:31
  71.9 0.0 copy-done
  71.9 2.1 %multiply_add_fusion.1 = f32[2,2,2,8192]{3,2,1,0:T(2,128)S(1)} fusion(bf16[2,17,2,8192]{3,2,1,0:T(2,128)(2,1)S(1)} %copy-done, f32[8192]{0:T(1024)S(1)} %get-tuple-element.19, f32[8192]{0:T(1024)S(1)} %get-tuple-element.20, f32[8192]{0:T(1024)S(1)} %get-tuple-element.21, f32[8192]{0:T(1024)S(1)} %get-tuple-element.22, f32[8192]{0:T(1024)S(1)} %get-tuple-element.23, ...), kind=kLoop, calls=%fused_computation.67 | loop fusion | flops 3080192 | bytes 2883584 | tf_op jit(solution)/shard_map/add | solution.py:51
  74.0 0.2 fusion.53
  74.2 0.2 copy_bitcast_fusion.1
  74.4 4.4 %add_convert_fusion = (bf16[16,2,2,1,8192]{4,3,2,1,0:T(2,128)(2,1)S(1)}, bf16[16,2,2,1,8192]{4,3,2,1,0:T(2,128)(2,1)S(1)}) fusion(f32[16,8192]{1,0:T(8,128)S(1)} %get-tuple-element.40, f32[2,2,8192]{2,1,0:T(2,128)S(1)} %get-tuple-element.38, f32[16,8192]{1,0:T(8,128)S(1)} %get-tuple-element.41, f32[2,2,8192]{2,1,0:T(2,128)S(1)} %get-tuple-element.39), kind=kLoop, calls=%fused_computation.23 | loop fusion | flops 4194304 | bytes 3407872 | tf_op jit(solution)/shard_map/convert
  78.8 4.8 %pad_maximum_fusion = bf16[16,2,2,2,8192]{4,3,2,1,0:T(2,128)(2,1)S(1)} fusion(bf16[16,2,2,1,8192]{4,3,2,1,0:T(2,128)(2,1)S(1)} %get-tuple-element.17, bf16[16,2,2,1,8192]{4,3,2,1,0:T(2,128)(2,1)S(1)} %get-tuple-element.16), kind=kLoop, calls=%fused_computation.21 | loop fusion | flops 4194304 | bytes 4194304 | tf_op jit(solution)/shard_map/stack | solution.py:58
  83.7 1.2 copy.55
  84.8 13.7 %fusion.19 = bf16[64,512]{1,0:T(8,128)(2,1)S(1)} fusion(bf16[64,16384]{1,0:T(8,128)(2,1)S(1)} %bitcast.50, bf16[8192,256]{1,0:T(8,128)(2,1)} %get-tuple-element.43, bf16[8192,256]{1,0:T(8,128)(2,1)} %get-tuple-element.42, bf16[8192,256]{1,0:T(8,128)(2,1)} %fusion.14), kind=kOutput, calls=%fused_computation.28 | convolution fusion | flops 1140916224 | bytes 14745600 | tf_op jit(solution)/shard_map/dot_general | solution.py:60
  98.6 4.9 %copy.50 = bf16[2,16,256,2,2]{4,3,0,2,1:T(2,128)(2,1)} copy(bf16[2,16,256,2,2]{2,1,4,3,0:T(8,128)(2,1)S(1)} %bitcast.51) | data formatting | bytes 131072 | tf_op jit(solution)/shard_map/reshape | solution.py:63
  103.6 7.8 %reshape.394 = bf16[4,2,4096]{2,1,0:T(2,128)(2,1)} reshape(bf16[4096,2,2,2]{3,2,1,0:T(2,128)(2,1)} %bitcast.46) | data formatting | bytes 131072
  111.3 4.3 %all-to-all-start = ((bf16[4,2,4096]{2,1,0:T(2,128)(2,1)}), bf16[4,2,4096]{2,1,0:T(2,128)(2,1)S(1)}, u32[]{:S(2)}, u32[]{:S(2)}) async-start(bf16[4,2,4096]{2,1,0:T(2,128)(2,1)} %reshape.394), calls=%async_computation | async-start | bytes 131072 | tf_op jit(solution)/shard_map/all_to_all | solution.py:95
  115.6 0.7 fusion.51
  116.3 0.7 compare_bitcast_fusion
  117.0 0.2 reduce-window.7
  117.2 0.2 select_reduce_fusion
  117.4 2.3 %all-to-all-done = bf16[4,2,4096]{2,1,0:T(2,128)(2,1)S(1)} async-done(((bf16[4,2,4096]{2,1,0:T(2,128)(2,1)}), bf16[4,2,4096]{2,1,0:T(2,128)(2,1)S(1)}, u32[]{:S(2)}, u32[]{:S(2)}) %all-to-all-start) | async-done | bytes 65568 | tf_op jit(solution)/shard_map/all_to_all | solution.py:95
  119.7 10.0 %reshape.395 = bf16[4096,2,2,2]{3,2,1,0:T(2,128)(2,1)} reshape(bf16[4,2,4096]{2,1,0:T(2,128)(2,1)S(1)} %all-to-all-done) | data formatting | bytes 131072
  129.7 9.7 %copy.51 = bf16[2,4,1024,2,2]{2,1,4,3,0:T(4,128)(2,1)S(1)} copy(bf16[2,4,1024,2,2]{4,3,0,2,1:T(2,128)(2,1)} %bitcast.47) | data formatting | bytes 131072 | tf_op jit(solution)/shard_map/all_to_all | solution.py:95
  139.5 0.1 copy.41
  139.6 2.0 %collective-permute-start = (bf16[1,8,1024,4]{2,1,3,0:T(8,128)(2,1)S(1)}, bf16[1,8,1024,4]{2,1,3,0:T(8,128)(2,1)S(1)}, u32[]{:S(2)}, u32[]{:S(2)}) collective-permute-start(bf16[1,8,1024,4]{2,1,3,0:T(8,128)(2,1)S(1)} %broadcast_in_dim_reshape.3), channel_id=1, source_target_pairs={{0,4},{4,8},{8,12},{12,16},{16,20},{20,24},{24,28},{28,0},{1,5},{5... | collective-permute-start | bytes 196616 | tf_op jit(solution)/shard_map/ppermute | solution.py:15
  141.6 5.3 %collective-permute-done = bf16[1,8,1024,4]{2,1,3,0:T(8,128)(2,1)S(1)} collective-permute-done((bf16[1,8,1024,4]{2,1,3,0:T(8,128)(2,1)S(1)}, bf16[1,8,1024,4]{2,1,3,0:T(8,128)(2,1)S(1)}, u32[]{:S(2)}, u32[]{:S(2)}) %collective-permute-start) | collective-permute-done | bytes 65568 | tf_op jit(solution)/shard_map/ppermute | solution.py:15
  146.9 0.1 collective-permute-start.1
  147.0 0.2 fusion.43
  147.2 0.1 broadcast_in_dim.75
  147.2 0.1 broadcast_in_dim.76
  147.3 0.1 broadcast_in_dim.70
  147.4 0.1 broadcast_in_dim.71
  147.5 2.6 %collective-permute-start.2 = (bf16[8,1024,4]{1,0,2:T(8,128)(2,1)S(1)}, bf16[8,1024,4]{1,0,2:T(8,128)(2,1)S(1)}, u32[]{:S(2)}, u32[]{:S(2)}) collective-permute-start(bf16[8,1024,4]{1,0,2:T(8,128)(2,1)S(1)} %reshape.350), channel_id=1, source_target_pairs={{0,16},{4,20},{8,24},{12,28},{16,0},{20,4},{24,8},{28,12},{1,17},{... | collective-permute-start | bytes 196616 | tf_op jit(solution)/shard_map/ppermute | solution.py:15
  150.1 1.4 copy.46
  151.5 4.0 %collective-permute-done.2 = bf16[8,1024,4]{1,0,2:T(8,128)(2,1)S(1)} collective-permute-done((bf16[8,1024,4]{1,0,2:T(8,128)(2,1)S(1)}, bf16[8,1024,4]{1,0,2:T(8,128)(2,1)S(1)}, u32[]{:S(2)}, u32[]{:S(2)}) %collective-permute-start.2) | collective-permute-done | bytes 65568 | tf_op jit(solution)/shard_map/ppermute | solution.py:15
  155.5 0.0 collective-permute-done.1
  155.5 1.4 copy.44
  157.0 1.4 copy.45
  158.4 3.8 %multiply_convert_fusion = bf16[1024,8,80]{2,1,0:T(8,128)(2,1)S(1)} fusion(bf16[8,1024,4]{0,2,1:T(4,128)(2,1)} %copy.46, bf16[40,1024,4]{0,2,1:T(4,128)(2,1)} %copy.45, bf16[40,1024,4]{0,2,1:T(4,128)(2,1)} %copy.44), kind=kOutput, calls=%fused_computation.20 | convolution fusion | flops 7864320 | bytes 2031616 | tf_op jit(solution)/shard_map/dot_general | solution.py:70
  162.2 2.0 %copy.47 = bf16[1024,8,80]{0,2,1:T(8,128)(2,1)S(1)} copy(bf16[1024,8,80]{2,1,0:T(8,128)(2,1)S(1)} %multiply_convert_fusion) | data formatting | bytes 2621440 | tf_op jit(solution)/shard_map/convert_element_type | solution.py:115
  164.2 0.1 copy.48
  164.3 0.6 gather_fusion
  165.0 1.5 fusion.15
  (13 shorter events, 0.3 us)
Async XLA Ops:
  39.5 32.4 %copy-start = (bf16[2,17,2,8192]{3,2,1,0:T(2,128)(2,1)S(1)}, bf16[2,17,2,8192]{3,2,1,0:T(2,128)(2,1)}, u32[]{:S(2)}) copy-start(bf16[2,17,2,8192]{3,2,1,0:T(2,128)(2,1)} %param.2) | copy-start | bytes 3342340
  111.3 8.4 %all-to-all-start = ((bf16[4,2,4096]{2,1,0:T(2,128)(2,1)}), bf16[4,2,4096]{2,1,0:T(2,128)(2,1)S(1)}, u32[]{:S(2)}, u32[]{:S(2)}) async-start(bf16[4,2,4096]{2,1,0:T(2,128)(2,1)} %reshape.394), calls=%async_computation | async-start | bytes 131072 | tf_op jit(solution)/shard_map/all_to_all | solution.py:95
  139.6 7.3 %collective-permute-start = (bf16[1,8,1024,4]{2,1,3,0:T(8,128)(2,1)S(1)}, bf16[1,8,1024,4]{2,1,3,0:T(8,128)(2,1)S(1)}, u32[]{:S(2)}, u32[]{:S(2)}) collective-permute-start(bf16[1,8,1024,4]{2,1,3,0:T(8,128)(2,1)S(1)} %broadcast_in_dim_reshape.3), channel_id=1, source_target_pairs={{0,4},{4,8},{8,12},{12,16},{16,20},{20,24},{24,28},{28,0},{1,5},{5... | collective-permute-start | bytes 196616 | tf_op jit(solution)/shard_map/ppermute | solution.py:15
  146.9 8.6 %collective-permute-start.1 = (bf16[2,8,1024,4]{2,1,3,0:T(8,128)(2,1)S(1)}, bf16[2,8,1024,4]{2,1,3,0:T(8,128)(2,1)S(1)}, u32[]{:S(2)}, u32[]{:S(2)}) collective-permute-start(bf16[2,8,1024,4]{2,1,3,0:T(8,128)(2,1)S(1)} %pad_maximum_fusion.3), channel_id=1, source_target_pairs={{0,8},{4,12},{8,16},{12,20},{16,24},{20,28},{24,0},{28,4},{1,9},{5... | collective-permute-start | bytes 393224 | tf_op jit(solution)/shard_map/ppermute | solution.py:15
  147.5 8.0 %collective-permute-start.2 = (bf16[8,1024,4]{1,0,2:T(8,128)(2,1)S(1)}, bf16[8,1024,4]{1,0,2:T(8,128)(2,1)S(1)}, u32[]{:S(2)}, u32[]{:S(2)}) collective-permute-start(bf16[8,1024,4]{1,0,2:T(8,128)(2,1)S(1)} %reshape.350), channel_id=1, source_target_pairs={{0,16},{4,20},{8,24},{12,28},{16,0},{20,4},{24,8},{28,12},{1,17},{... | collective-permute-start | bytes 196616 | tf_op jit(solution)/shard_map/ppermute | solution.py:15
where the time goes:
time: 167 us; the launch traced here: 166 us
  other arithmetic  86.7 us (52%)
  local copies, waits for them, and re-layouts  41.5 us (25%)
  matrix products  17.5 us (10%)
  waiting for transfers between devices  11.6 us (7%)
  starting transfers between devices  8.94 us (5%)
    convert_element_type x1, other arithmetic, twiddles(): sines = jnp.sin(phase).astype(jnp.bfloat16)  35 us
    neg x1, other arithmetic, twiddles(): upper = jnp.concatenate([cosines, -sines], axis=1)  32.3 us
    unnamed x6, local copies, waits for them, and re-layouts  19.2 us
    dot_general x1, matrix products, channelise(): jnp.dot(lhs, table, preferred_element_type=jnp.float32)  13.7 us
    all_to_all x2, local copies, waits for them, and re-layouts, per_device(): lax.all_to_all(spectrum, 'chan', split_axis=1, concat_axis=0, tiled=True)  9.8 us
    ppermute x3, waiting for transfers between devices, from_behind(): lax.ppermute(value, axis, [(i, (i + by) % devices) for i in range(devices)])  9.25 us
    reshape x1, local copies, waits for them, and re-layouts, channelise(): return spectrum.reshape(count, ch_tot, 2, frames)  4.94 us
    another operation x1, other arithmetic, channelise(): lhs = jnp.stack([rot_real, rot_imag], axis=3).astype(jnp.bfloat16)  4.84 us
  transfers between devices with their start and end apart: 4, of which 3 were waited for; matrix products, arithmetic and copies ran while one was open for 2% of the time, Pallas kernels for 0%

commit v1 on v0

--- a/solution.py
+++ b/solution.py
@@ -8,6 +8,20 @@
 TAPS = 16
 CH_WIN = 1024
 DFT_BLOCK = 256
+
+
+def assign_turns(arr, dim_k, message):
+    reply, even = (arr.shape[:dim_k], arr.shape[dim_k + 1 :])
+    mixed_arr = arr.reshape(*reply, message, -1, *even)
+    return jnp.moveaxis(mixed_arr, dim_k, 0)
+
+
+def supply_all_space(frame, dim_at):
+    frame = jnp.moveaxis(frame, 0, dim_at)
+    t_next = frame.shape
+    return frame.reshape(
+        *t_next[:dim_at], t_next[dim_at] * t_next[dim_at + 1], *t_next[dim_at + 2 :]
+    )
 
 
 def from_behind(value, axis, by):
@@ -92,7 +106,19 @@
     frames = samples.shape[1] - TAPS + 1
     cos_rot, sin_rot = rotations(ch_tot, DFT_BLOCK)
     spectrum = channelise(samples, taps_table(), twiddles(DFT_BLOCK), cos_rot, sin_rot, ch_tot)
-    local = lax.all_to_all(spectrum, "chan", split_axis=1, concat_axis=0, tiled=True)
+    inter = lax.axis_index("chan")
+    after = lax.axis_size("chan")
+    block_next, kept_arr = (after, inter)
+    met_up = assign_turns(spectrum, 1, block_next)
+    spare = met_up
+    for s in [*range(1, block_next)]:
+        block_now, newest = ((kept_arr + s) % block_next, (kept_arr - s) % block_next)
+        long_array = lax.dynamic_index_in_dim(met_up, block_now, 0)
+        base_arr = lax.ppermute(
+            long_array, "chan", [(p, (p + s) % block_next) for p in range(block_next)]
+        )
+        spare = lax.dynamic_update_slice_in_dim(spare, base_arr, newest, axis=0)
+    local = supply_all_space(spare, 0)
     group_in = local.shape[0]
     own = local.reshape(group_in, CH_WIN, 2 * frames)
     keep_slots = n_stn // 2 + 1

time: 167 us -> 133 us (0.80)
  local copies, waits for them, and re-layouts: 41.5 us -> 9.68 us
  waiting for transfers between devices: 11.6 us -> 9.77 us
    unnamed x6 -> x4, local copies, waits for them, and re-layouts: 19.2 us -> 1.37 us
    all_to_all x2 -> x0, local copies, waits for them, and re-layouts: 9.8 us -> none  [per_device(): lax.all_to_all(spectrum, 'chan', split_axis=1, concat_axis=0, tiled=True)]
    reshape x3 -> x0, local copies, waits for them, and re-layouts: 6.33 us -> none  [the longest x1 4.94 us: channelise(): return spectrum.reshape(count, ch_tot, 2, frames)]
    ppermute x0 -> x3, starting transfers between devices: none -> 4.51 us  [per_device(): lax.ppermute(long_array, 'chan', [(p, (p + s) % block_next) for p in rang...]
    all_to_all x1 -> x0, starting transfers between devices: 4.26 us -> none  [per_device(): lax.all_to_all(spectrum, 'chan', split_axis=1, concat_axis=0, tiled=True)]
    all_to_all x1 -> x0, waiting for transfers between devices: 2.33 us -> none  [per_device(): lax.all_to_all(spectrum, 'chan', split_axis=1, concat_axis=0, tiled=True)]
  transfers between devices with their start and end apart: 4 -> 6, of which waited for: 3 -> 2; matrix products, arithmetic and copies ran while one was open for 2% -> 3% of each run, Pallas kernels for 0% -> 0%
where the time goes in v1:
time: 133 us
  other arithmetic  86.8 us (65%)
  matrix products  17.5 us (13%)
  waiting for transfers between devices  9.77 us (7%)
  local copies, waits for them, and re-layouts  9.68 us (7%)
  starting transfers between devices  8.53 us (6%)
    convert_element_type x1, other arithmetic, twiddles(): sines = jnp.sin(phase).astype(jnp.bfloat16)  35.1 us
    neg x1, other arithmetic, twiddles(): upper = jnp.concatenate([cosines, -sines], axis=1)  32.4 us
    dot_general x1, matrix products, channelise(): jnp.dot(lhs, table, preferred_element_type=jnp.float32)  13.7 us
    ppermute x3, waiting for transfers between devices, from_behind(): lax.ppermute(value, axis, [(i, (i + by) % devices) for i in range(devices)])  9.77 us
    another operation x1, other arithmetic, channelise(): lhs = jnp.stack([rot_real, rot_imag], axis=3).astype(jnp.bfloat16)  4.84 us
    another operation x2, other arithmetic  4.58 us
    ppermute x3, starting transfers between devices, per_device(): lax.ppermute(long_array, 'chan', [(p, (p + s) % block_next) for p in rang...  4.51 us
    ppermute x3, starting transfers between devices, from_behind(): lax.ppermute(value, axis, [(i, (i + by) % devices) for i in range(devices)])  4.02 us
  transfers between devices with their start and end apart: 6, of which 2 were waited for; matrix products, arithmetic and copies ran while one was open for 3% of the time, Pallas kernels for 0%

profile of v1, /device:TPU:0, one launch (start us, length us, event | category | flops | bytes accessed | tf_op | source)
XLA Modules:
  0.0 132.6 jit_solution(797827355461149321)
XLA Ops:
  0.0 2.4 %fusion.29 = f32[131072]{0:T(1024)S(1)} fusion(), kind=kLoop, calls=%fused_computation.45 | loop fusion | flops 5373952 | bytes 524288 | tf_op jit(solution)/shard_map/mul | solution.py:36
  2.4 2.1 %fusion.41 = (f32[16,8192]{1,0:T(8,128)S(1)}, f32[16,8192]{1,0:T(8,128)S(1)}) fusion(), kind=kLoop, calls=%fused_computation.65 | loop fusion | flops 1966080 | bytes 1048576 | tf_op jit(solution)/shard_map/sin | solution.py:55
  4.5 35.1 %sine_convert_fusion = (bf16[8192,256]{1,0:T(8,128)(2,1)}, bf16[8192,256]{1,0:T(8,128)(2,1)}) fusion(), kind=kLoop, calls=%fused_computation.15 | loop fusion | flops 33554432 | bytes 8388608 | tf_op jit(solution)/shard_map/convert_element_type | solution.py:44
  39.5 0.0 copy-start
  39.5 32.4 %fusion.14 = bf16[8192,256]{1,0:T(8,128)(2,1)} fusion(), kind=kLoop, calls=%fused_computation.24 | loop fusion | flops 37748736 | bytes 4194304 | tf_op jit(solution)/shard_map/neg | solution.py:45
  71.9 0.0 copy-done
  71.9 2.1 %multiply_add_fusion.1 = f32[2,2,2,8192]{3,2,1,0:T(2,128)S(1)} fusion(bf16[2,17,2,8192]{3,2,1,0:T(2,128)(2,1)S(1)} %copy-done, f32[8192]{0:T(1024)S(1)} %get-tuple-element.19, f32[8192]{0:T(1024)S(1)} %get-tuple-element.20, f32[8192]{0:T(1024)S(1)} %get-tuple-element.21, f32[8192]{0:T(1024)S(1)} %get-tuple-element.22, f32[8192]{0:T(1024)S(1)} %get-tuple-element.23, ...), kind=kLoop, calls=%fused_computation.67 | loop fusion | flops 3080192 | bytes 2883584 | tf_op jit(solution)/shard_map/add | solution.py:65
  74.0 0.2 fusion.53
  74.2 0.2 copy_bitcast_fusion.1
  74.5 4.4 %add_convert_fusion = (bf16[16,2,2,1,8192]{4,3,2,1,0:T(2,128)(2,1)S(1)}, bf16[16,2,2,1,8192]{4,3,2,1,0:T(2,128)(2,1)S(1)}) fusion(f32[16,8192]{1,0:T(8,128)S(1)} %get-tuple-element.43, f32[2,2,8192]{2,1,0:T(2,128)S(1)} %get-tuple-element.41, f32[16,8192]{1,0:T(8,128)S(1)} %get-tuple-element.44, f32[2,2,8192]{2,1,0:T(2,128)S(1)} %get-tuple-element.42), kind=kLoop, calls=%fused_computation.23 | loop fusion | flops 4194304 | bytes 3407872 | tf_op jit(solution)/shard_map/convert
  78.9 4.8 %pad_maximum_fusion = bf16[16,2,2,2,8192]{4,3,2,1,0:T(2,128)(2,1)S(1)} fusion(bf16[16,2,2,1,8192]{4,3,2,1,0:T(2,128)(2,1)S(1)} %get-tuple-element.17, bf16[16,2,2,1,8192]{4,3,2,1,0:T(2,128)(2,1)S(1)} %get-tuple-element.16), kind=kLoop, calls=%fused_computation.21 | loop fusion | flops 4194304 | bytes 4194304 | tf_op jit(solution)/shard_map/stack | solution.py:72
  83.7 1.2 copy.49
  84.9 13.7 %fusion.19 = bf16[64,512]{1,0:T(8,128)(2,1)S(1)} fusion(bf16[64,16384]{1,0:T(8,128)(2,1)S(1)} %bitcast.54, bf16[8192,256]{1,0:T(8,128)(2,1)} %get-tuple-element.46, bf16[8192,256]{1,0:T(8,128)(2,1)} %get-tuple-element.45, bf16[8192,256]{1,0:T(8,128)(2,1)} %fusion.14), kind=kOutput, calls=%fused_computation.28 | convolution fusion | flops 1140916224 | bytes 14745600 | tf_op jit(solution)/shard_map/dot_general | solution.py:74
  98.7 0.1 dynamic-slice_bitcast_fusion
  98.8 0.5 collective-permute-start
  99.4 2.6 %collective-permute-start.1 = (bf16[1,2,1024,2,2]{2,0,4,3,1:T(2,128)(2,1)S(1)}, bf16[1,2,1024,2,2]{2,0,4,3,1:T(2,128)(2,1)S(1)}, u32[]{:S(2)}, u32[]{:S(2)}) collective-permute-start(bf16[1,2,1024,2,2]{2,0,4,3,1:T(2,128)(2,1)S(1)} %get-tuple-element.39), channel_id=1, source_target_pairs={{0,2},{1,3},{2,0},{3,1},{4,6},{5,7},{6,4},{7,5},{8,10},{9,11},{10,... | collective-permute-start | bytes 49160 | tf_op jit(solution)/shard_map/ppermute | solution.py:117
  101.9 1.4 %collective-permute-start.2 = (bf16[1,2,1024,2,2]{2,0,4,3,1:T(2,128)(2,1)S(1)}, bf16[1,2,1024,2,2]{2,0,4,3,1:T(2,128)(2,1)S(1)}, u32[]{:S(2)}, u32[]{:S(2)}) collective-permute-start(bf16[1,2,1024,2,2]{2,0,4,3,1:T(2,128)(2,1)S(1)} %get-tuple-element.38), channel_id=1, source_target_pairs={{0,3},{1,0},{2,1},{3,2},{4,7},{5,4},{6,5},{7,6},{8,11},{9,8},{10,9... | collective-permute-start | bytes 49160 | tf_op jit(solution)/shard_map/ppermute | solution.py:117
  103.3 0.7 fusion.51
  104.0 0.7 compare_bitcast_fusion
  104.7 0.2 reduce-window.7
  104.9 0.2 select_reduce_fusion
  105.2 0.0 collective-permute-done
  105.2 0.2 dynamic_update_slice.9
  105.4 0.0 collective-permute-done.1
  105.4 0.2 dynamic_update_slice.10
  105.6 0.0 collective-permute-done.2
  105.6 0.2 dynamic_update_slice.11
  105.7 0.1 copy.37
  105.9 1.5 %collective-permute-start.3 = (bf16[1,8,1024,4]{2,1,3,0:T(8,128)(2,1)S(1)}, bf16[1,8,1024,4]{2,1,3,0:T(8,128)(2,1)S(1)}, u32[]{:S(2)}, u32[]{:S(2)}) collective-permute-start(bf16[1,8,1024,4]{2,1,3,0:T(8,128)(2,1)S(1)} %broadcast_in_dim_reshape_reshape.3), channel_id=1, source_target_pairs={{0,4},{4,8},{8,12},{12,16},{16,20},{20,24},{24,28},{28,0},{1,5},{5... | collective-permute-start | bytes 196616 | tf_op jit(solution)/shard_map/ppermute | solution.py:29
  107.4 5.5 %collective-permute-done.3 = bf16[1,8,1024,4]{2,1,3,0:T(8,128)(2,1)S(1)} collective-permute-done((bf16[1,8,1024,4]{2,1,3,0:T(8,128)(2,1)S(1)}, bf16[1,8,1024,4]{2,1,3,0:T(8,128)(2,1)S(1)}, u32[]{:S(2)}, u32[]{:S(2)}) %collective-permute-start.3) | collective-permute-done | bytes 65568 | tf_op jit(solution)/shard_map/ppermute | solution.py:29
  112.9 0.1 collective-permute-start.4
  113.0 0.2 fusion.43
  113.1 0.1 broadcast_in_dim.75
  113.2 0.1 broadcast_in_dim.76
  113.3 0.1 broadcast_in_dim.70
  113.4 0.1 broadcast_in_dim.71
  113.5 2.4 %collective-permute-start.5 = (bf16[8,1024,4]{1,0,2:T(8,128)(2,1)S(1)}, bf16[8,1024,4]{1,0,2:T(8,128)(2,1)S(1)}, u32[]{:S(2)}, u32[]{:S(2)}) collective-permute-start(bf16[8,1024,4]{1,0,2:T(8,128)(2,1)S(1)} %reshape_reshape.7), channel_id=1, source_target_pairs={{0,16},{4,20},{8,24},{12,28},{16,0},{20,4},{24,8},{28,12},{1,17},{... | collective-permute-start | bytes 196616 | tf_op jit(solution)/shard_map/ppermute | solution.py:29
  115.9 1.4 %copy.42 = bf16[8,1024,4]{0,2,1:T(4,128)(2,1)} copy(bf16[8,1024,4]{1,0,2:T(8,128)(2,1)S(1)} %reshape_reshape.7) | data formatting | bytes 131072 | tf_op jit(solution)/shard_map/reshape;reshape | solution.py:123
  117.3 4.3 %collective-permute-done.5 = bf16[8,1024,4]{1,0,2:T(8,128)(2,1)S(1)} collective-permute-done((bf16[8,1024,4]{1,0,2:T(8,128)(2,1)S(1)}, bf16[8,1024,4]{1,0,2:T(8,128)(2,1)S(1)}, u32[]{:S(2)}, u32[]{:S(2)}) %collective-permute-start.5) | collective-permute-done | bytes 65568 | tf_op jit(solution)/shard_map/ppermute | solution.py:29
  121.6 0.0 collective-permute-done.4
  121.7 1.4 %copy.40 = bf16[40,1024,4]{0,2,1:T(4,128)(2,1)} copy(bf16[40,1024,4]{1,0,2:T(8,128)(2,1)S(1)} %copy_bitcast_fusion) | data formatting | bytes 655360 | tf_op jit(solution)/shard_map/reshape | solution.py:140
  123.1 1.4 %copy.41 = bf16[40,1024,4]{0,2,1:T(4,128)(2,1)} copy(bf16[40,1024,4]{1,0,2:T(8,128)(2,1)S(1)} %pad_maximum_fusion.2) | data formatting | bytes 655360 | tf_op jit(solution)/shard_map/concatenate | solution.py:82
  124.5 3.8 %multiply_convert_fusion = bf16[1024,8,80]{2,1,0:T(8,128)(2,1)S(1)} fusion(bf16[8,1024,4]{0,2,1:T(4,128)(2,1)} %copy.42, bf16[40,1024,4]{0,2,1:T(4,128)(2,1)} %copy.41, bf16[40,1024,4]{0,2,1:T(4,128)(2,1)} %copy.40), kind=kOutput, calls=%fused_computation.20 | convolution fusion | flops 7864320 | bytes 2031616 | tf_op jit(solution)/shard_map/dot_general | solution.py:84
  128.3 2.0 %copy.43 = bf16[1024,8,80]{0,2,1:T(8,128)(2,1)S(1)} copy(bf16[1024,8,80]{2,1,0:T(8,128)(2,1)S(1)} %multiply_convert_fusion) | data formatting | bytes 2621440 | tf_op jit(solution)/shard_map/convert_element_type | solution.py:141
  130.3 0.1 copy.44
  130.4 0.6 gather_fusion
  131.1 1.5 %fusion.15 = bf16[8,2,1024,40]{2,3,1,0:T(8,128)(2,1)} fusion(pred[40]{0:T(512)(128)(4,1)S(1)} %broadcast_in_dim.76, pred[40]{0:T(512)(128)(4,1)S(1)} %broadcast_in_dim.71, bf16[5,8,2,1024,8]{3,4,2,1,0:T(8,128)(2,1)S(1)} %gather_fusion), kind=kLoop, calls=%fused_computation.26 | loop fusion | flops 1310720 | bytes 2621520 | tf_op jit(solution)/shard_map/jit(_where)/select_n | solution.py:145
  (14 shorter events, 0.3 us)
Async XLA Ops:
  39.5 32.4 %copy-start = (bf16[2,17,2,8192]{3,2,1,0:T(2,128)(2,1)S(1)}, bf16[2,17,2,8192]{3,2,1,0:T(2,128)(2,1)}, u32[]{:S(2)}) copy-start(bf16[2,17,2,8192]{3,2,1,0:T(2,128)(2,1)} %param.2) | copy-start | bytes 3342340
  98.8 6.4 %collective-permute-start = (bf16[1,2,1024,2,2]{2,0,4,3,1:T(2,128)(2,1)S(1)}, bf16[1,2,1024,2,2]{2,0,4,3,1:T(2,128)(2,1)S(1)}, u32[]{:S(2)}, u32[]{:S(2)}) collective-permute-start(bf16[1,2,1024,2,2]{2,0,4,3,1:T(2,128)(2,1)S(1)} %get-tuple-element.40), channel_id=1, source_target_pairs={{0,1},{1,2},{2,3},{3,0},{4,5},{5,6},{6,7},{7,4},{8,9},{9,10},{10,1... | collective-permute-start | bytes 49160 | tf_op jit(solution)/shard_map/ppermute | solution.py:117
  99.4 6.0 %collective-permute-start.1 = (bf16[1,2,1024,2,2]{2,0,4,3,1:T(2,128)(2,1)S(1)}, bf16[1,2,1024,2,2]{2,0,4,3,1:T(2,128)(2,1)S(1)}, u32[]{:S(2)}, u32[]{:S(2)}) collective-permute-start(bf16[1,2,1024,2,2]{2,0,4,3,1:T(2,128)(2,1)S(1)} %get-tuple-element.39), channel_id=1, source_target_pairs={{0,2},{1,3},{2,0},{3,1},{4,6},{5,7},{6,4},{7,5},{8,10},{9,11},{10,... | collective-permute-start | bytes 49160 | tf_op jit(solution)/shard_map/ppermute | solution.py:117
  101.9 3.6 %collective-permute-start.2 = (bf16[1,2,1024,2,2]{2,0,4,3,1:T(2,128)(2,1)S(1)}, bf16[1,2,1024,2,2]{2,0,4,3,1:T(2,128)(2,1)S(1)}, u32[]{:S(2)}, u32[]{:S(2)}) collective-permute-start(bf16[1,2,1024,2,2]{2,0,4,3,1:T(2,128)(2,1)S(1)} %get-tuple-element.38), channel_id=1, source_target_pairs={{0,3},{1,0},{2,1},{3,2},{4,7},{5,4},{6,5},{7,6},{8,11},{9,8},{10,9... | collective-permute-start | bytes 49160 | tf_op jit(solution)/shard_map/ppermute | solution.py:117
  105.9 7.0 %collective-permute-start.3 = (bf16[1,8,1024,4]{2,1,3,0:T(8,128)(2,1)S(1)}, bf16[1,8,1024,4]{2,1,3,0:T(8,128)(2,1)S(1)}, u32[]{:S(2)}, u32[]{:S(2)}) collective-permute-start(bf16[1,8,1024,4]{2,1,3,0:T(8,128)(2,1)S(1)} %broadcast_in_dim_reshape_reshape.3), channel_id=1, source_target_pairs={{0,4},{4,8},{8,12},{12,16},{16,20},{20,24},{24,28},{28,0},{1,5},{5... | collective-permute-start | bytes 196616 | tf_op jit(solution)/shard_map/ppermute | solution.py:29
  112.9 8.7 %collective-permute-start.4 = (bf16[2,8,1024,4]{2,1,3,0:T(8,128)(2,1)S(1)}, bf16[2,8,1024,4]{2,1,3,0:T(8,128)(2,1)S(1)}, u32[]{:S(2)}, u32[]{:S(2)}) collective-permute-start(bf16[2,8,1024,4]{2,1,3,0:T(8,128)(2,1)S(1)} %pad_maximum_fusion.3), channel_id=1, source_target_pairs={{0,8},{4,12},{8,16},{12,20},{16,24},{20,28},{24,0},{28,4},{1,9},{5... | collective-permute-start | bytes 393224 | tf_op jit(solution)/shard_map/ppermute | solution.py:29
  113.5 8.1 %collective-permute-start.5 = (bf16[8,1024,4]{1,0,2:T(8,128)(2,1)S(1)}, bf16[8,1024,4]{1,0,2:T(8,128)(2,1)S(1)}, u32[]{:S(2)}, u32[]{:S(2)}) collective-permute-start(bf16[8,1024,4]{1,0,2:T(8,128)(2,1)S(1)} %reshape_reshape.7), channel_id=1, source_target_pairs={{0,16},{4,20},{8,24},{12,28},{16,0},{20,4},{24,8},{28,12},{1,17},{... | collective-permute-start | bytes 196616 | tf_op jit(solution)/shard_map/ppermute | solution.py:29
